TPU v7x, 128 devices: a whole 4x4x4 slice. The times are simulated.
128 devices in a mesh: rows: 8 (over y_hi, x), feat: 16 (over y_lo, z, core).
Axes of the slice: x: 4, y: 4 (y_hi: 2, y_lo: 2; y = y_hi * 2 + y_lo), z: 4, core: 2. Of those that a mesh axis runs over, the one named last changes fastest.
Arguments:
- bins: int32 [768, 32768], P('feat', 'rows'), may hold values from 0 to 255
- fold: int32 [32768], P('rows'), may hold values from 0 to 9
- nodes: int32 [32768, 10], P('rows'), may hold values from 0 to 3
- gradient: bfloat16 [32768], P('rows'), may hold values from -6 to 6
- hessian: bfloat16 [32768], P('rows'), may hold values from 0.049804688 to 1
Outputs:
- train_hist: float32 [80, 768, 256], P('rows', 'feat')
- node_gain: float32 [10, 4], replicated
All inputs are finite; a program needn't handle non-finite values.
Results may differ from a plain program's by a relative error of at most 0.0003.
Values sent between devices are 32-bit elements; how exact they have to be, the bound alone decides.
A program may use at most 64 MiB of HBM per device.

v0:
```python
import jax
import jax.numpy as jnp
from jax import lax
from jax.sharding import PartitionSpec as P

BINS = 256
FOLDS = 10
NODES = 4


def from_everyone(shard, axis):
    copies = jnp.broadcast_to(shard, (lax.axis_size(axis), *shard.shape))
    return lax.all_to_all(copies, axis, split_axis=0, concat_axis=0, tiled=True)


def taken_together(shard, axis):
    everything = from_everyone(shard, axis)
    return jnp.max(everything, axis=0)


def accumulate(bins, weights):
    feats, rows_here = bins.shape
    block = min(512, rows_here)
    group = min(16, feats)
    columns = weights.shape[0]
    levels = jnp.arange(BINS, dtype=jnp.int32)[:, None]

    def visit(turn, total):
        start = turn * block
        part_bins = lax.dynamic_slice_in_dim(bins, start, block, 1)
        part_weights = lax.dynamic_slice_in_dim(weights, start, block, 1)
        for first in range(0, feats, group):
            onehot = (part_bins[first : first + group, None, :] == levels[None]).astype(
                jnp.bfloat16
            )
            term = jnp.einsum(
                "cr,fbr->cfb", part_weights, onehot, preferred_element_type=jnp.float32
            )
            total = total.at[:, first : first + group].add(term)
        return total

    empty = jnp.zeros((columns, feats, BINS), jnp.float32)
    return lax.fori_loop(0, rows_here // block, visit, empty)


def on_device(bins, fold, nodes, gradient, hessian):
    feats, rows_here = bins.shape
    grad = gradient.astype(jnp.float32)[:, None]
    hess = hessian.astype(jnp.float32)[:, None]
    kept = (fold[:, None] != jnp.arange(FOLDS, dtype=jnp.int32)[None, :])[:, :, None]
    node_hot = nodes[:, :, None] == jnp.arange(NODES, dtype=jnp.int32)[None, None, :]
    selected = (node_hot & kept).reshape(rows_here, FOLDS * NODES).astype(jnp.float32)
    weights = jnp.stack([grad * selected, hess * selected], axis=2).reshape(
        rows_here, FOLDS * NODES * 2
    )
    weights = weights.T.astype(jnp.bfloat16)
    local = accumulate(bins, weights)
    reduced = lax.psum_scatter(local, "rows", scatter_dimension=0, tiled=True)
    owned = reduced.shape[0] // 2
    split = reduced.reshape(owned, 2, feats, BINS)
    totals = jnp.sum(split[:, :, 0, :], axis=-1)
    running = jnp.cumsum(split, axis=-1)
    left_g, left_h = (running[:, 0], running[:, 1])
    whole_g = totals[:, 0][:, None, None]
    whole_h = totals[:, 1][:, None, None]
    gain = (
        left_g * left_g / (left_h + 1.0)
        + (whole_g - left_g) ** 2 / (whole_h - left_h + 1.0)
        - whole_g * whole_g / (whole_h + 1.0)
    )
    level = jnp.arange(BINS, dtype=jnp.int32)[None, None, :]
    gain = jnp.where(level < BINS - 1, gain, -1e30)
    mine = jnp.max(gain, axis=(1, 2))
    filled = jnp.full((FOLDS * NODES,), -1e30, jnp.float32)
    best = lax.dynamic_update_slice_in_dim(filled, mine, lax.axis_index("rows") * owned, 0)
    best = taken_together(best, "rows")
    best = taken_together(best, "feat")
    return (reduced, best.reshape(FOLDS, NODES))


def solution(mesh):
    in_specs = (P("feat", "rows"), P("rows"), P("rows", None), P("rows"), P("rows"))
    out_specs = (P("rows", "feat", None), P())
    return jax.shard_map(
        on_device, mesh=mesh, in_specs=in_specs, out_specs=out_specs, check_vma=False
    )
```

profile of v0, /device:TPU:1, one launch (start us, length us, event | category | flops | bytes accessed | tf_op | source)
XLA Modules:
  0.0 254.6 jit_solution(15556475086000980698)
XLA Ops:
  7.2 0.0 copy-start
  7.2 0.0 reduce-scatter.2.cloned.1.call-start
  7.2 1.1 eq.142
  8.3 0.2 eq.143
  8.5 0.8 iota_compare_fusion.18
  9.3 0.2 and.52
  9.5 0.1 and.53
  9.6 0.1 eq.145
  9.7 0.9 select_convert_fusion.1
  10.6 0.0 copy-done
  10.6 0.1 select_convert_fusion
  10.7 0.1 pad_maximum_fusion
  10.8 0.7 copy.39
  11.5 0.2 convert_element_type.25
  11.7 2.4 broadcast_in_dim.39
  14.1 107.2 %while.21 = (s32[]{:T(128)}, f32[80,48,256]{2,0,1:T(8,128)}, bf16[80,4096]{1,0:T(8,128)(2,1)S(1)}, s32[48,4096]{1,0:T(8,128)}, s32[]{:T(128)}, /*index=5*/s32[]{:T(128)}, s32[]{}, s32[]{:T(128)}, s32[]{:T(128)}, s32[]{}) while((s32[]{:T(128)}, f32[80,48,256]{2,0,1:T(8,128)}, bf16[80,4096]{1,0:T(8,128)(2,1)S(1)}, ...), condition=%wide.region_1.2_spmd.clone.clone, body=%wide.region_0.1_spmd.clone.clone.sunk | while | flops 1013907456 | bytes 8405187 | solution.py:43
  14.1 0.8 fusion.34
  14.9 4.2 %fusion.35 = f32[80,48,256]{2,0,1:T(8,128)} fusion(f32[80,48,256]{2,0,1:T(8,128)} %get-tuple-element.328, s32[16,512]{1,0:T(8,128)S(1)} %get-tuple-element.314, bf16[80,4096]{1,0:T(8,128)(2,1)S(1)} %get-tuple-element.339, s32[]{:T(128)S(6)} %select_n.25), kind=kOutput, calls=%fused_computation.15.clone.1 | convolution fusion | flops 337969152 | bytes 2736132 | tf_op jit(solution)/shard_map/while/body/eval_jaxpr/cr,fbr->cfb/dot_general | solution.py:36
  19.1 4.2 %fusion.36 = f32[80,48,256]{2,0,1:T(8,128)} fusion(f32[80,48,256]{2,0,1:T(8,128)} %fusion.35, s32[16,512]{1,0:T(8,128)S(1)} %get-tuple-element.315, bf16[80,4096]{1,0:T(8,128)(2,1)S(1)} %get-tuple-element.339, s32[]{:T(128)S(6)} %select_n.25), kind=kOutput, calls=%fused_computation.13.clone.1 | convolution fusion | flops 337969152 | bytes 2736132 | tf_op jit(solution)/shard_map/while/body/eval_jaxpr/cr,fbr->cfb/dot_general | solution.py:36
  23.3 4.2 %fusion.37 = f32[80,48,256]{2,0,1:T(8,128)} fusion(f32[80,48,256]{2,0,1:T(8,128)} %fusion.36, s32[16,512]{1,0:T(8,128)S(1)} %get-tuple-element.316, bf16[80,4096]{1,0:T(8,128)(2,1)S(1)} %get-tuple-element.339, s32[]{:T(128)S(6)} %select_n.25), kind=kOutput, calls=%fused_computation.11.clone.1 | convolution fusion | flops 337969152 | bytes 2736132 | tf_op jit(solution)/shard_map/while/body/eval_jaxpr/cr,fbr->cfb/dot_general | solution.py:36
  27.5 0.8 fusion.34
  28.3 4.2 %fusion.35 = f32[80,48,256]{2,0,1:T(8,128)} fusion(f32[80,48,256]{2,0,1:T(8,128)} %get-tuple-element.328, s32[16,512]{1,0:T(8,128)S(1)} %get-tuple-element.314, bf16[80,4096]{1,0:T(8,128)(2,1)S(1)} %get-tuple-element.339, s32[]{:T(128)S(6)} %select_n.25), kind=kOutput, calls=%fused_computation.15.clone.1 | convolution fusion | flops 337969152 | bytes 2736132 | tf_op jit(solution)/shard_map/while/body/eval_jaxpr/cr,fbr->cfb/dot_general | solution.py:36
  32.5 4.2 %fusion.36 = f32[80,48,256]{2,0,1:T(8,128)} fusion(f32[80,48,256]{2,0,1:T(8,128)} %fusion.35, s32[16,512]{1,0:T(8,128)S(1)} %get-tuple-element.315, bf16[80,4096]{1,0:T(8,128)(2,1)S(1)} %get-tuple-element.339, s32[]{:T(128)S(6)} %select_n.25), kind=kOutput, calls=%fused_computation.13.clone.1 | convolution fusion | flops 337969152 | bytes 2736132 | tf_op jit(solution)/shard_map/while/body/eval_jaxpr/cr,fbr->cfb/dot_general | solution.py:36
  36.7 4.2 %fusion.37 = f32[80,48,256]{2,0,1:T(8,128)} fusion(f32[80,48,256]{2,0,1:T(8,128)} %fusion.36, s32[16,512]{1,0:T(8,128)S(1)} %get-tuple-element.316, bf16[80,4096]{1,0:T(8,128)(2,1)S(1)} %get-tuple-element.339, s32[]{:T(128)S(6)} %select_n.25), kind=kOutput, calls=%fused_computation.11.clone.1 | convolution fusion | flops 337969152 | bytes 2736132 | tf_op jit(solution)/shard_map/while/body/eval_jaxpr/cr,fbr->cfb/dot_general | solution.py:36
  40.9 0.8 fusion.34
  41.7 4.2 %fusion.35 = f32[80,48,256]{2,0,1:T(8,128)} fusion(f32[80,48,256]{2,0,1:T(8,128)} %get-tuple-element.328, s32[16,512]{1,0:T(8,128)S(1)} %get-tuple-element.314, bf16[80,4096]{1,0:T(8,128)(2,1)S(1)} %get-tuple-element.339, s32[]{:T(128)S(6)} %select_n.25), kind=kOutput, calls=%fused_computation.15.clone.1 | convolution fusion | flops 337969152 | bytes 2736132 | tf_op jit(solution)/shard_map/while/body/eval_jaxpr/cr,fbr->cfb/dot_general | solution.py:36
  45.9 4.2 %fusion.36 = f32[80,48,256]{2,0,1:T(8,128)} fusion(f32[80,48,256]{2,0,1:T(8,128)} %fusion.35, s32[16,512]{1,0:T(8,128)S(1)} %get-tuple-element.315, bf16[80,4096]{1,0:T(8,128)(2,1)S(1)} %get-tuple-element.339, s32[]{:T(128)S(6)} %select_n.25), kind=kOutput, calls=%fused_computation.13.clone.1 | convolution fusion | flops 337969152 | bytes 2736132 | tf_op jit(solution)/shard_map/while/body/eval_jaxpr/cr,fbr->cfb/dot_general | solution.py:36
  50.1 4.2 %fusion.37 = f32[80,48,256]{2,0,1:T(8,128)} fusion(f32[80,48,256]{2,0,1:T(8,128)} %fusion.36, s32[16,512]{1,0:T(8,128)S(1)} %get-tuple-element.316, bf16[80,4096]{1,0:T(8,128)(2,1)S(1)} %get-tuple-element.339, s32[]{:T(128)S(6)} %select_n.25), kind=kOutput, calls=%fused_computation.11.clone.1 | convolution fusion | flops 337969152 | bytes 2736132 | tf_op jit(solution)/shard_map/while/body/eval_jaxpr/cr,fbr->cfb/dot_general | solution.py:36
  54.3 0.8 fusion.34
  55.1 4.2 %fusion.35 = f32[80,48,256]{2,0,1:T(8,128)} fusion(f32[80,48,256]{2,0,1:T(8,128)} %get-tuple-element.328, s32[16,512]{1,0:T(8,128)S(1)} %get-tuple-element.314, bf16[80,4096]{1,0:T(8,128)(2,1)S(1)} %get-tuple-element.339, s32[]{:T(128)S(6)} %select_n.25), kind=kOutput, calls=%fused_computation.15.clone.1 | convolution fusion | flops 337969152 | bytes 2736132 | tf_op jit(solution)/shard_map/while/body/eval_jaxpr/cr,fbr->cfb/dot_general | solution.py:36
  59.3 4.2 %fusion.36 = f32[80,48,256]{2,0,1:T(8,128)} fusion(f32[80,48,256]{2,0,1:T(8,128)} %fusion.35, s32[16,512]{1,0:T(8,128)S(1)} %get-tuple-element.315, bf16[80,4096]{1,0:T(8,128)(2,1)S(1)} %get-tuple-element.339, s32[]{:T(128)S(6)} %select_n.25), kind=kOutput, calls=%fused_computation.13.clone.1 | convolution fusion | flops 337969152 | bytes 2736132 | tf_op jit(solution)/shard_map/while/body/eval_jaxpr/cr,fbr->cfb/dot_general | solution.py:36
  63.5 4.2 %fusion.37 = f32[80,48,256]{2,0,1:T(8,128)} fusion(f32[80,48,256]{2,0,1:T(8,128)} %fusion.36, s32[16,512]{1,0:T(8,128)S(1)} %get-tuple-element.316, bf16[80,4096]{1,0:T(8,128)(2,1)S(1)} %get-tuple-element.339, s32[]{:T(128)S(6)} %select_n.25), kind=kOutput, calls=%fused_computation.11.clone.1 | convolution fusion | flops 337969152 | bytes 2736132 | tf_op jit(solution)/shard_map/while/body/eval_jaxpr/cr,fbr->cfb/dot_general | solution.py:36
  67.7 0.8 fusion.34
  68.5 4.2 %fusion.35 = f32[80,48,256]{2,0,1:T(8,128)} fusion(f32[80,48,256]{2,0,1:T(8,128)} %get-tuple-element.328, s32[16,512]{1,0:T(8,128)S(1)} %get-tuple-element.314, bf16[80,4096]{1,0:T(8,128)(2,1)S(1)} %get-tuple-element.339, s32[]{:T(128)S(6)} %select_n.25), kind=kOutput, calls=%fused_computation.15.clone.1 | convolution fusion | flops 337969152 | bytes 2736132 | tf_op jit(solution)/shard_map/while/body/eval_jaxpr/cr,fbr->cfb/dot_general | solution.py:36
  72.7 4.2 %fusion.36 = f32[80,48,256]{2,0,1:T(8,128)} fusion(f32[80,48,256]{2,0,1:T(8,128)} %fusion.35, s32[16,512]{1,0:T(8,128)S(1)} %get-tuple-element.315, bf16[80,4096]{1,0:T(8,128)(2,1)S(1)} %get-tuple-element.339, s32[]{:T(128)S(6)} %select_n.25), kind=kOutput, calls=%fused_computation.13.clone.1 | convolution fusion | flops 337969152 | bytes 2736132 | tf_op jit(solution)/shard_map/while/body/eval_jaxpr/cr,fbr->cfb/dot_general | solution.py:36
  76.9 4.2 %fusion.37 = f32[80,48,256]{2,0,1:T(8,128)} fusion(f32[80,48,256]{2,0,1:T(8,128)} %fusion.36, s32[16,512]{1,0:T(8,128)S(1)} %get-tuple-element.316, bf16[80,4096]{1,0:T(8,128)(2,1)S(1)} %get-tuple-element.339, s32[]{:T(128)S(6)} %select_n.25), kind=kOutput, calls=%fused_computation.11.clone.1 | convolution fusion | flops 337969152 | bytes 2736132 | tf_op jit(solution)/shard_map/while/body/eval_jaxpr/cr,fbr->cfb/dot_general | solution.py:36
  81.1 0.8 fusion.34
  81.9 4.2 %fusion.35 = f32[80,48,256]{2,0,1:T(8,128)} fusion(f32[80,48,256]{2,0,1:T(8,128)} %get-tuple-element.328, s32[16,512]{1,0:T(8,128)S(1)} %get-tuple-element.314, bf16[80,4096]{1,0:T(8,128)(2,1)S(1)} %get-tuple-element.339, s32[]{:T(128)S(6)} %select_n.25), kind=kOutput, calls=%fused_computation.15.clone.1 | convolution fusion | flops 337969152 | bytes 2736132 | tf_op jit(solution)/shard_map/while/body/eval_jaxpr/cr,fbr->cfb/dot_general | solution.py:36
  86.1 4.2 %fusion.36 = f32[80,48,256]{2,0,1:T(8,128)} fusion(f32[80,48,256]{2,0,1:T(8,128)} %fusion.35, s32[16,512]{1,0:T(8,128)S(1)} %get-tuple-element.315, bf16[80,4096]{1,0:T(8,128)(2,1)S(1)} %get-tuple-element.339, s32[]{:T(128)S(6)} %select_n.25), kind=kOutput, calls=%fused_computation.13.clone.1 | convolution fusion | flops 337969152 | bytes 2736132 | tf_op jit(solution)/shard_map/while/body/eval_jaxpr/cr,fbr->cfb/dot_general | solution.py:36
  90.3 4.2 %fusion.37 = f32[80,48,256]{2,0,1:T(8,128)} fusion(f32[80,48,256]{2,0,1:T(8,128)} %fusion.36, s32[16,512]{1,0:T(8,128)S(1)} %get-tuple-element.316, bf16[80,4096]{1,0:T(8,128)(2,1)S(1)} %get-tuple-element.339, s32[]{:T(128)S(6)} %select_n.25), kind=kOutput, calls=%fused_computation.11.clone.1 | convolution fusion | flops 337969152 | bytes 2736132 | tf_op jit(solution)/shard_map/while/body/eval_jaxpr/cr,fbr->cfb/dot_general | solution.py:36
  94.5 0.8 fusion.34
  95.3 4.2 %fusion.35 = f32[80,48,256]{2,0,1:T(8,128)} fusion(f32[80,48,256]{2,0,1:T(8,128)} %get-tuple-element.328, s32[16,512]{1,0:T(8,128)S(1)} %get-tuple-element.314, bf16[80,4096]{1,0:T(8,128)(2,1)S(1)} %get-tuple-element.339, s32[]{:T(128)S(6)} %select_n.25), kind=kOutput, calls=%fused_computation.15.clone.1 | convolution fusion | flops 337969152 | bytes 2736132 | tf_op jit(solution)/shard_map/while/body/eval_jaxpr/cr,fbr->cfb/dot_general | solution.py:36
  99.5 4.2 %fusion.36 = f32[80,48,256]{2,0,1:T(8,128)} fusion(f32[80,48,256]{2,0,1:T(8,128)} %fusion.35, s32[16,512]{1,0:T(8,128)S(1)} %get-tuple-element.315, bf16[80,4096]{1,0:T(8,128)(2,1)S(1)} %get-tuple-element.339, s32[]{:T(128)S(6)} %select_n.25), kind=kOutput, calls=%fused_computation.13.clone.1 | convolution fusion | flops 337969152 | bytes 2736132 | tf_op jit(solution)/shard_map/while/body/eval_jaxpr/cr,fbr->cfb/dot_general | solution.py:36
  103.7 4.2 %fusion.37 = f32[80,48,256]{2,0,1:T(8,128)} fusion(f32[80,48,256]{2,0,1:T(8,128)} %fusion.36, s32[16,512]{1,0:T(8,128)S(1)} %get-tuple-element.316, bf16[80,4096]{1,0:T(8,128)(2,1)S(1)} %get-tuple-element.339, s32[]{:T(128)S(6)} %select_n.25), kind=kOutput, calls=%fused_computation.11.clone.1 | convolution fusion | flops 337969152 | bytes 2736132 | tf_op jit(solution)/shard_map/while/body/eval_jaxpr/cr,fbr->cfb/dot_general | solution.py:36
  107.9 0.8 fusion.34
  108.7 4.2 %fusion.35 = f32[80,48,256]{2,0,1:T(8,128)} fusion(f32[80,48,256]{2,0,1:T(8,128)} %get-tuple-element.328, s32[16,512]{1,0:T(8,128)S(1)} %get-tuple-element.314, bf16[80,4096]{1,0:T(8,128)(2,1)S(1)} %get-tuple-element.339, s32[]{:T(128)S(6)} %select_n.25), kind=kOutput, calls=%fused_computation.15.clone.1 | convolution fusion | flops 337969152 | bytes 2736132 | tf_op jit(solution)/shard_map/while/body/eval_jaxpr/cr,fbr->cfb/dot_general | solution.py:36
  112.9 4.2 %fusion.36 = f32[80,48,256]{2,0,1:T(8,128)} fusion(f32[80,48,256]{2,0,1:T(8,128)} %fusion.35, s32[16,512]{1,0:T(8,128)S(1)} %get-tuple-element.315, bf16[80,4096]{1,0:T(8,128)(2,1)S(1)} %get-tuple-element.339, s32[]{:T(128)S(6)} %select_n.25), kind=kOutput, calls=%fused_computation.13.clone.1 | convolution fusion | flops 337969152 | bytes 2736132 | tf_op jit(solution)/shard_map/while/body/eval_jaxpr/cr,fbr->cfb/dot_general | solution.py:36
  117.1 4.2 %fusion.37 = f32[80,48,256]{2,0,1:T(8,128)} fusion(f32[80,48,256]{2,0,1:T(8,128)} %fusion.36, s32[16,512]{1,0:T(8,128)S(1)} %get-tuple-element.316, bf16[80,4096]{1,0:T(8,128)(2,1)S(1)} %get-tuple-element.339, s32[]{:T(128)S(6)} %select_n.25), kind=kOutput, calls=%fused_computation.11.clone.1 | convolution fusion | flops 337969152 | bytes 2736132 | tf_op jit(solution)/shard_map/while/body/eval_jaxpr/cr,fbr->cfb/dot_general | solution.py:36
  121.3 6.3 %copy.40 = f32[80,48,256]{2,1,0:T(8,128)} copy(f32[80,48,256]{2,0,1:T(8,128)} %get-tuple-element.231) | data formatting | bytes 7864320 | tf_op jit(solution)/shard_map/while | solution.py:43
  127.6 0.0 reduce-scatter.2.cloned.1.call-update
  127.6 85.9 %reduce-scatter.2.cloned.1.call-done = f32[10,48,256]{2,1,0:T(8,128)} async-done(((f32[80,48,256]{2,1,0:T(8,128)}), f32[10,48,256]{2,1,0:T(8,128)}) %reduce-scatter.2.cloned.1.call-update) | async-done | bytes 491536 | tf_op jit(solution)/shard_map/reduce_scatter | solution.py:58
  213.5 1.0 slice_reduce_fusion.1
  214.5 0.2 slice_reduce_fusion.3
  214.7 1.3 reshape.394
  216.0 5.9 %reduce-window.6 = f32[5,2,48,2,128]{4,2,3,1,0:T(8,128)S(1)} reduce-window(f32[5,2,48,2,128]{4,2,3,1,0:T(8,128)S(1)} %copy.41, f32[]{:T(128)} %constant.236.clone.1), window={size=1x1x1x1x128 pad=0_0x0_0x0_0x0_0x127_0}, to_apply=%region_3.4 | reduce-window | flops 15605760 | bytes 983044 | tf_op jit(solution)/shard_map/reduce-window
  221.9 0.4 slice_reduce_fusion
  222.3 0.2 copy_bitcast_fusion
  222.5 0.2 select_reduce_fusion
  222.8 0.2 dynamic_update_slice.8
  223.0 9.3 %all_to_all.12 = f32[8,1,40]{2,1,0:T(1,128)S(1)} all-to-all(f32[8,1,40]{2,1,0:T(1,128)S(1)} %broadcast_in_dim.42), channel_id=1, replica_groups=mesh['rows'=8,'feat'=16] {'rows'}, dimensions={0} | all-to-all | bytes 2560 | tf_op jit(solution)/shard_map/all_to_all | solution.py:13
  232.4 14.6 %all_to_all.13 = f32[16,1,40]{2,1,0:T(1,128)S(1)} all-to-all(f32[16,1,40]{2,1,0:T(1,128)S(1)} %broadcast_in_dim.43), channel_id=1, replica_groups=mesh['rows'=8,'feat'=16] {'feat'}, dimensions={0} | all-to-all | bytes 5120 | tf_op jit(solution)/shard_map/all_to_all | solution.py:13
  247.0 0.1 reshape.397
  247.0 0.7 copy.46
  (11 shorter events, 0.2 us)
Async XLA Ops:
  7.2 3.5 %copy-start = (bf16[4096]{0:T(1024)(128)(2,1)S(1)}, bf16[4096]{0:T(1024)(128)(2,1)}, u32[]{:S(2)}) copy-start(bf16[4096]{0:T(1024)(128)(2,1)} %param.17) | copy-start | bytes 24580
  7.2 206.3 %reduce-scatter.2.cloned.1.call-start = ((), (), s32[]{:S(2)}) async-start(), calls=%async_computation.3 | async-start | bytes 4423680 | tf_op jit(solution)/shard_map/reduce_scatter | solution.py:58
Sparse Core Ops, SparseCore 0:
  127.7 85.7 reduce-scatter.1
where the time goes:
time: 256 us; the launch traced here: 255 us
  matrix products  101 us (39%)
  waiting for transfers between devices  85.9 us (34%)
  blocking collectives  23.9 us (9%)
  local copies, waits for them, and re-layouts  20.5 us (8%)
  between operations  14.2 us (6%)
  other arithmetic  9.27 us (4%)
    dot_general x24, matrix products, visit(): jnp.einsum('cr,fbr->cfb', part_weights, onehot, preferred_element_type=jn...  101 us
    reduce_scatter x1, waiting for transfers between devices, on_device(): reduced = lax.psum_scatter(local, 'rows', scatter_dimension=0, tiled=True)  85.9 us
    all_to_all x2, blocking collectives, from_everyone(): return lax.all_to_all(copies, axis, split_axis=0, concat_axis=0, tiled=True)  23.9 us
    another operation x5, other arithmetic  7.16 us
    slice x8, local copies, waits for them, and re-layouts, visit(): part_bins[first:first + group, None, :] == levels[None]  6.37 us
    while x1, local copies, waits for them, and re-layouts, accumulate(): return lax.fori_loop(0, rows_here // block, visit, empty)  6.29 us
  transfers between devices with their start and end apart: 1, of which 1 were waited for; matrix products, arithmetic and copies ran while one was open for 0% of the time, Pallas kernels for 0%

commit v1 on v0

v1 whole, which is shorter than its diff:
```python
import functools

import jax
import jax.numpy as jnp
from jax import lax
from jax.experimental import pallas as pl
from jax.experimental.pallas import tpu as pltpu
from jax.sharding import PartitionSpec as P

BINS = 256
FOLDS = 10
NODES = 4
COLS = FOLDS * NODES * 2
X = 4
Y = 2
OWN = COLS // (X * Y)
NF = 4
BLK = OWN * NF
CUT = 24
F8 = jnp.float8_e4m3fn
MESH = pl.DeviceIdType.MESH
LOW = -1e30
LANES = 128
HALVES = BINS // LANES
KC = 512


def build_weights(fold_ref, nodes_ref, grad_ref, hess_ref, w_ref):
    rows = w_ref.shape[1]
    grad = grad_ref[...].astype(jnp.float32)
    hess = hess_ref[...].astype(jnp.float32)
    biggest = jnp.max(jnp.abs(grad), axis=1, keepdims=True)
    up = jnp.full((1, 1), 64.0, jnp.float32)
    down = jnp.full((1, 1), 1.0 / 64.0, jnp.float32)
    for e in (32, 16, 8, 4, 2, 1):
        fits = biggest * up * (2.0**e) <= 448.0
        up = jnp.where(fits, up * (2.0**e), up)
        down = jnp.where(fits, down * (2.0**-e), down)
    line = lax.broadcasted_iota(jnp.int32, (8, KC), 0)
    for at in range(0, rows, KC):
        g = grad[:, at : at + KC] * up
        h = hess[:, at : at + KC] * 256.0
        both = jnp.where(line % 2 == 0, jnp.broadcast_to(g, (8, KC)), jnp.broadcast_to(h, (8, KC)))
        first = both.astype(F8).astype(jnp.float32)
        second = (both - first) * 16.0
        fold = fold_ref[:, at : at + KC]
        pieces = [[], []]
        for k in range(FOLDS):
            node = nodes_ref[k : k + 1, at : at + KC]
            node = jnp.where(fold == k, -1, node)
            sel = jnp.broadcast_to(node, (8, KC)) == line // 2
            pieces[0].append(jnp.where(sel, first, 0.0))
            pieces[1].append(jnp.where(sel, second, 0.0))
        every = pieces[0] + pieces[1]
        for q in range(0, 2 * FOLDS, 4):
            w_ref[q * 8 : q * 8 + 32, at : at + KC] = jnp.concatenate(every[q : q + 4], axis=0).astype(F8)
    return down


def histogram(bins_ref, w_ref, loc_ref, slot, first, scale):
    rows = w_ref.shape[1]
    level = lax.broadcasted_iota(jnp.int32, (BINS, 1), 0).astype(jnp.float32).astype(jnp.bfloat16)
    for f in range(NF):
        total = None
        for at in range(0, rows, KC):
            b = bins_ref[pl.ds(first + f, 1), at : at + KC].astype(jnp.float32).astype(jnp.bfloat16)
            hot = jnp.where(b == level, jnp.bfloat16(1), jnp.bfloat16(0)).astype(F8)
            term = lax.dot_general(
                w_ref[:, at : at + KC], hot, (((1,), (1,)), ((), ())), preferred_element_type=jnp.float32
            )
            total = term if total is None else total + term
        hist = (total[:COLS] + total[COLS:] * (1.0 / 16.0)) * scale
        for part in range(HALVES):
            loc_ref[slot, part, pl.ds(f, COLS, stride=NF), :] = hist[:, part * LANES : (part + 1) * LANES]


def gains(done):
    lane = lax.broadcasted_iota(jnp.int32, (BLK, BINS), 1)
    line = lax.broadcasted_iota(jnp.int32, (BLK, BINS), 0)
    left = done
    step = 1
    while step < BINS:
        left = left + jnp.where(lane >= step, pltpu.roll(left, step, 1), 0.0)
        step *= 2
    whole = jnp.broadcast_to(left[:, BINS - 1 :], (BLK, BINS))
    left_h = pltpu.roll(left, BLK - NF, 0)
    whole_h = pltpu.roll(whole, BLK - NF, 0)
    good = (line % (2 * NF) < NF) & (lane < BINS - 1)
    left_h = jnp.where(good, left_h, 0.0)
    whole_h = jnp.where(good, whole_h, 0.0)
    gain = (
        left * left / (left_h + 1.0)
        + (whole - left) * (whole - left) / (whole_h - left_h + 1.0)
        - whole * whole / (whole_h + 1.0)
    )
    return jnp.where(good, gain, LOW)


def kernel(
    pairs, feats_way,
    bins_ref, fold_ref, nodes_ref, grad_ref, hess_ref,
    hist_ref, best_ref,
    w_ref, locx, locy, r1, r2, r3, y1, y2, y3, most, near_out, near_in, far_in,
    xs, xr, ys, yr, ns, nr, fs, fr,
):
    row = lax.axis_index("rows")
    feat = lax.axis_index("feat")
    y, x = row // X, row % X
    around = X * Y

    barrier = pltpu.get_barrier_semaphore()

    def greet_rows(d, c):
        pl.semaphore_signal(barrier, inc=1, device_id={"rows": (row + d) % around}, device_id_type=MESH)
        return c

    def greet_feats(d, c):
        pl.semaphore_signal(barrier, inc=1, device_id={"feat": (feat + d) % feats_way}, device_id_type=MESH)
        return c

    lax.fori_loop(1, around, greet_rows, 0)
    lax.fori_loop(1, feats_way, greet_feats, 0)

    right = {"rows": y * X + (x + 1) % X}
    left = {"rows": y * X + (x + X - 1) % X}
    over = {"rows": (Y - 1 - y) * X + x}

    def spot(yy, xx, start=0):
        return pl.multiple_of((yy * X + xx % X) * BLK + start, 8)

    def send(src, dst, sems, at, k, to):
        return pltpu.make_async_remote_copy(
            src_ref=src, dst_ref=dst, send_sem=sems[0].at[at, k], recv_sem=sems[1].at[at, k],
            device_id=to, device_id_type=MESH,
        )

    def x_copy(i, k):
        def blk(yy, xx):
            return locx.at[i, :, pl.ds(spot(yy, xx), BLK)]

        src, dst, to = (
            lambda: (blk(0, x + 2), r1.at[i, 0], right),
            lambda: (blk(1, x + 2), r1.at[i, 1], left),
            lambda: (blk(1, x + 1), r2.at[i, 1], right),
            lambda: (blk(0, x + 3), r2.at[i, 2], left),
            lambda: (blk(0, x + 1), r2.at[i, 0], right),
            lambda: (blk(1, x + 3), r2.at[i, 3], left),
            lambda: (blk(Y - 1 - y, x), r3.at[i], over),
        )[k]()
        return send(src, dst, (xs, xr), i, k, to)

    def y_copy(i, k):
        def part(xx, a, b):
            return locy.at[i, :, pl.ds(spot(y, xx, a), b - a)]

        def into(ref, a, b):
            return ref.at[:, pl.ds(a, b - a)]

        src, dst, to = (
            lambda: (locy.at[i, :, pl.ds(spot(Y - 1 - y, 0), X * BLK)], y1.at[i], over),
            lambda: (part(x + 2, 0, CUT), into(y2.at[i], 0, CUT), right),
            lambda: (part(x + 2, CUT, BLK), into(y2.at[i], CUT, BLK), left),
            lambda: (part(x + 1, CUT, BLK), into(y3.at[i, 0], CUT, BLK), right),
            lambda: (part(x + 3, 0, CUT), into(y3.at[i, 1], 0, CUT), left),
            lambda: (part(x + 1, 0, CUT), into(y3.at[i, 0], 0, CUT), right),
            lambda: (part(x + 3, CUT, BLK), into(y3.at[i, 1], CUT, BLK), left),
        )[k]()
        return send(src, dst, (ys, yr), i, k, to)

    down = build_weights(fold_ref, nodes_ref, grad_ref, hess_ref, w_ref)
    column = lax.broadcasted_iota(jnp.int32, (COLS, BINS), 0)
    scale = jnp.where(column % 2 == 0, jnp.broadcast_to(down, (COLS, BINS)), 1.0 / 256.0)
    most[...] = jnp.full(most.shape, LOW, jnp.float32)

    def visit(i, carry):
        @pl.when(i < pairs)
        def _():
            histogram(bins_ref, w_ref, locx, i, 2 * NF * i, scale)

            @pl.when(i == 0)
            def _():
                pl.semaphore_wait(barrier, around - 1 + feats_way - 1)

            for k in range(4):
                x_copy(i, k).start()
            histogram(bins_ref, w_ref, locy, i, 2 * NF * i + NF, scale)
            y_copy(i, 0).start()

        @pl.when((i >= 1) & (i < pairs + 1))
        def _():
            j = i - 1
            x_copy(j, 0).wait_recv()
            x_copy(j, 1).wait_recv()
            locx[j, :, pl.ds(spot(0, x + 1), BLK), :] += r1[j, 0]
            locx[j, :, pl.ds(spot(1, x + 3), BLK), :] += r1[j, 1]
            x_copy(j, 4).start()
            x_copy(j, 5).start()
            y_copy(j, 0).wait_recv()
            locy[j, :, pl.ds(spot(y, 0), X * BLK), :] += y1[j]
            for k in range(1, 5):
                y_copy(j, k).start()

        @pl.when((i >= 2) & (i < pairs + 2))
        def _():
            j = i - 2
            for k in range(2, 6):
                x_copy(j, k).wait_recv()
            locx[j, :, pl.ds(spot(0, x), BLK), :] += r2[j, 0] + r2[j, 2]
            locx[j, :, pl.ds(spot(1, x), BLK), :] += r2[j, 1] + r2[j, 3]
            x_copy(j, 6).start()
            y_copy(j, 1).wait_recv()
            y_copy(j, 2).wait_recv()
            locy[j, :, pl.ds(spot(y, x + 1), CUT), :] += y2[j, :, pl.ds(0, CUT), :]
            locy[j, :, pl.ds(spot(y, x + 3, CUT), BLK - CUT), :] += y2[j, :, pl.ds(CUT, BLK - CUT), :]
            y_copy(j, 5).start()
            y_copy(j, 6).start()

        @pl.when(i >= 3)
        def _():
            j = i - 3
            x_copy(j, 6).wait_recv()
            done_x = locx[j, :, pl.ds(spot(y, x), BLK), :] + r3[j]
            for k in range(3, 7):
                y_copy(j, k).wait_recv()
            done_y = locy[j, :, pl.ds(spot(y, x), BLK), :] + y3[j, 0] + y3[j, 1]
            done_x = jnp.concatenate([done_x[h] for h in range(HALVES)], axis=1)
            done_y = jnp.concatenate([done_y[h] for h in range(HALVES)], axis=1)
            for c in range(OWN):
                hist_ref[c, pl.ds(pl.multiple_of(2 * NF * j, 2 * NF), 2 * NF), :] = jnp.concatenate(
                    [done_x[c * NF : (c + 1) * NF], done_y[c * NF : (c + 1) * NF]], axis=0
                )
            most[...] = jnp.maximum(most[...], jnp.maximum(gains(done_x), gains(done_y)))

        return carry

    lax.fori_loop(0, pairs + 3, visit, 0)

    def settle(i, carry):
        for k in range(7):
            x_copy(i, k).wait_send()
            y_copy(i, k).wait_send()
        return carry

    lane = lax.broadcasted_iota(jnp.int32, (8, 128), 1)
    mine = jnp.full((8, 128), LOW, jnp.float32)
    for m in range(OWN // 2):
        part = most[m * 2 * NF : (m + 1) * 2 * NF, :]
        part = jnp.max(jnp.max(part, axis=1, keepdims=True), axis=0, keepdims=True)
        mine = jnp.where(lane == row * (OWN // 2) + m, jnp.broadcast_to(part, (8, 128)), mine)
    near_out[0] = mine

    def near(d):
        return pltpu.make_async_remote_copy(
            src_ref=near_out.at[0], dst_ref=near_in.at[d], send_sem=ns.at[d], recv_sem=nr.at[d],
            device_id={"feat": (feat + d) % feats_way}, device_id_type=MESH,
        )

    def far(d):
        return pltpu.make_async_remote_copy(
            src_ref=near_out.at[1], dst_ref=far_in.at[d], send_sem=fs.at[d], recv_sem=fr.at[d],
            device_id={"rows": (row + d) % around}, device_id_type=MESH,
        )

    for d in range(1, feats_way):
        near(d).start()
    lax.fori_loop(0, pairs, settle, 0)
    for d in range(1, feats_way):
        near(d).wait_recv()
        mine = jnp.maximum(mine, near_in[d])
    near_out[1] = mine
    for d in range(1, around):
        far(d).start()
    for d in range(1, around):
        far(d).wait_recv()
        mine = jnp.maximum(mine, far_in[d])
    for k in range(FOLDS):
        best_ref[k : k + 1, :] = mine[0:1, k * NODES : (k + 1) * NODES]
    for d in range(1, feats_way):
        near(d).wait_send()
    for d in range(1, around):
        far(d).wait_send()


def on_device(bins, fold, nodes, gradient, hessian):
    feats, rows_here = bins.shape
    pairs = feats // (2 * NF)
    feats_way = lax.axis_size("feat")
    around = X * Y
    f32 = jnp.float32
    dma = pltpu.SemaphoreType.DMA
    vmem = pl.BlockSpec(memory_space=pltpu.VMEM)
    return pl.pallas_call(
        functools.partial(kernel, pairs, feats_way),
        out_shape=(
            jax.ShapeDtypeStruct((OWN, feats, BINS), f32),
            jax.ShapeDtypeStruct((FOLDS, NODES), f32),
        ),
        in_specs=[vmem] * 5,
        out_specs=(vmem, vmem),
        scratch_shapes=[
            pltpu.VMEM((2 * COLS, rows_here), F8),
            pltpu.VMEM((pairs, HALVES, COLS * NF, LANES), f32),
            pltpu.VMEM((pairs, HALVES, COLS * NF, LANES), f32),
            pltpu.VMEM((pairs, 2, HALVES, BLK, LANES), f32),
            pltpu.VMEM((pairs, 4, HALVES, BLK, LANES), f32),
            pltpu.VMEM((pairs, HALVES, BLK, LANES), f32),
            pltpu.VMEM((pairs, HALVES, X * BLK, LANES), f32),
            pltpu.VMEM((pairs, HALVES, BLK, LANES), f32),
            pltpu.VMEM((pairs, 2, HALVES, BLK, LANES), f32),
            pltpu.VMEM((BLK, BINS), f32),
            pltpu.VMEM((2, 8, 128), f32),
            pltpu.VMEM((feats_way, 8, 128), f32),
            pltpu.VMEM((around, 8, 128), f32),
            dma((pairs, 7)), dma((pairs, 7)), dma((pairs, 7)), dma((pairs, 7)),
            dma((feats_way,)), dma((feats_way,)), dma((around,)), dma((around,)),
        ],
        compiler_params=pltpu.CompilerParams(
            collective_id=0, has_side_effects=True, vmem_limit_bytes=48 << 20
        ),
    )(bins, fold.reshape(1, -1), nodes.T, gradient.reshape(1, -1), hessian.reshape(1, -1))


def solution(mesh):
    in_specs = (P("feat", "rows"), P("rows"), P("rows", None), P("rows"), P("rows"))
    out_specs = (P("rows", "feat", None), P())
    return jax.shard_map(
        on_device, mesh=mesh, in_specs=in_specs, out_specs=out_specs, check_vma=False
    )
```

time: 256 us -> 61.7 us (0.24)
  matrix products: 101 us -> 0 us
  waiting for transfers between devices: 85.9 us -> 0 us
  Pallas kernels: 0 us -> 55.8 us
  blocking collectives: 23.9 us -> 0 us
  local copies, waits for them, and re-layouts: 20.5 us -> 4.94 us
  between operations: 14.2 us -> 0.68 us
  other arithmetic: 9.27 us -> 0 us
    dot_general x24 -> x0, matrix products: 101 us -> none  [visit(): jnp.einsum('cr,fbr->cfb', part_weights, onehot, preferred_element_type=jn...]
    reduce_scatter x1 -> x0, waiting for transfers between devices: 85.9 us -> none  [on_device(): reduced = lax.psum_scatter(local, 'rows', scatter_dimension=0, tiled=True)]
    pallas_call x0 -> x1, Pallas kernels: none -> 55.8 us  [on_device(): pl.pallas_call(functools.partial(kernel, pairs, feats_way), out_shape=(ja...]
    all_to_all x2 -> x0, blocking collectives: 23.9 us -> none  [from_everyone(): return lax.all_to_all(copies, axis, split_axis=0, concat_axis=0, tiled=True)]
    another operation x6 -> x0, other arithmetic: 7.22 us -> none
    slice x9 -> x0, local copies, waits for them, and re-layouts: 6.55 us -> none  [the longest x8 6.37 us: visit(): part_bins[first:first + group, None, :] == levels[None]]
    while x1 -> x0, local copies, waits for them, and re-layouts: 6.29 us -> none  [accumulate(): return lax.fori_loop(0, rows_here // block, visit, empty)]
    unnamed x3 -> x9, local copies, waits for them, and re-layouts: 0.68 us -> 3.56 us
  transfers between devices with their start and end apart: 1 -> 0, of which waited for: 1 -> 0; matrix products, arithmetic and copies ran while one was open for 0% -> 0% of each run, Pallas kernels for 0% -> 0%
where the time goes in v1:
time: 61.7 us; the launch traced here: 61.4 us
  Pallas kernels  55.8 us (90%)
  local copies, waits for them, and re-layouts  4.94 us (8%)
  between operations  0.68 us (1%)
    pallas_call x1, Pallas kernels, on_device(): pl.pallas_call(functools.partial(kernel, pairs, feats_way), out_shape=(ja...  55.8 us
    unnamed x9, local copies, waits for them, and re-layouts  3.56 us

profile of v1, /device:TPU:1, one launch (start us, length us, event | category | flops | bytes accessed | tf_op | source)
XLA Modules:
  0.0 61.4 jit_solution(8510207756938295018)
XLA Ops:
  0.6 0.0 copy-start.3
  0.6 0.7 %reshape.14.grad_ref = bf16[1,4096]{1,0:T(2,128)(2,1)S(1)} reshape(bf16[4096]{0:T(1024)(128)(2,1)} %param.8) | data formatting | bytes 16384 | tf_op jit(solution)/shard_map/reshape | solution.py:320
  1.4 0.0 copy-done.3
  1.4 0.0 copy-start.2
  1.4 0.7 %copy-done.2 = s32[4096]{0:T(1024)S(1)} copy-done((s32[4096]{0:T(1024)S(1)}, s32[4096]{0:T(1024)}, u32[]{:S(2)}) %copy-start.2) | copy-done | bytes 16408
  2.1 0.0 copy-start
  2.1 1.1 %copy-done = s32[48,4096]{1,0:T(8,128)S(1)} copy-done((s32[48,4096]{1,0:T(8,128)S(1)}, s32[48,4096]{1,0:T(8,128)}, u32[]{:S(2)}) %copy-start) | copy-done | bytes 786456
  3.2 0.0 copy-start.1
  3.2 0.9 %copy-done.1 = s32[4096,10]{0,1:T(8,128)S(1)} copy-done((s32[4096,10]{0,1:T(8,128)S(1)}, s32[4096,10]{0,1:T(8,128)}, u32[]{:S(2)}) %copy-start.1) | copy-done | bytes 163864
  4.2 55.8 %shard_map.68 = (f32[10,48,256]{2,1,0:T(8,128)S(1)}, f32[10,4]{1,0:T(8,128)S(1)}) custom-call(s32[48,4096]{1,0:T(8,128)S(1)} %copy-done, s32[1,4096]{1,0:T(1,128)S(1)} %bitcast.3, s32[10,4096]{1,0:T(8,128)S(1)} %bitcast.2, bf16[1,4096]{1,0:T(2,128)(2,1)S(1)} %reshape.14.grad_ref, bf16[1,4096]{1,0:T(2,128)(2,1)S(1)} %reshape.15.hess_ref), custom_call_target="tpu_custom_call" | custom-call | tf_op jit(solution)/shard_map/pallas_call | solution.py:292
  59.9 0.7 %copy.7 = f32[10,4]{0,1:T(4,128)} copy(f32[10,4]{1,0:T(8,128)S(1)} %get-tuple-element.3) | data formatting | bytes 320 | tf_op jit(solution)/shard_map/pallas_call | solution.py:292
  60.6 0.8 %copy.9 = f32[10,48,256]{2,1,0:T(8,128)} copy(f32[10,48,256]{2,1,0:T(8,128)S(1)} %get-tuple-element.6) | data formatting | bytes 983040
  (1 shorter events, 0.0 us)
Async XLA Ops:
  0.6 0.7 %copy-start.3 = (bf16[4096]{0:T(1024)(128)(2,1)S(1)}, bf16[4096]{0:T(1024)(128)(2,1)}, u32[]{:S(2)}) copy-start(bf16[4096]{0:T(1024)(128)(2,1)} %param.9) | copy-start | bytes 24580
  1.4 0.7 %copy-start.2 = (s32[4096]{0:T(1024)S(1)}, s32[4096]{0:T(1024)}, u32[]{:S(2)}) copy-start(s32[4096]{0:T(1024)} %param.6) | copy-start | bytes 49156
  2.1 1.1 %copy-start = (s32[48,4096]{1,0:T(8,128)S(1)}, s32[48,4096]{1,0:T(8,128)}, u32[]{:S(2)}) copy-start(s32[48,4096]{1,0:T(8,128)} %bins_ref.1) | copy-start | bytes 2359300
  3.2 0.9 %copy-start.1 = (s32[4096,10]{0,1:T(8,128)S(1)}, s32[4096,10]{0,1:T(8,128)}, u32[]{:S(2)}) copy-start(s32[4096,10]{0,1:T(8,128)} %param.7) | copy-start | bytes 491524

commit v2 on v1

--- a/solution.py
+++ b/solution.py
@@ -27,37 +27,21 @@
 
 def build_weights(fold_ref, nodes_ref, grad_ref, hess_ref, w_ref):
     rows = w_ref.shape[1]
-    grad = grad_ref[...].astype(jnp.float32)
-    hess = hess_ref[...].astype(jnp.float32)
-    biggest = jnp.max(jnp.abs(grad), axis=1, keepdims=True)
-    up = jnp.full((1, 1), 64.0, jnp.float32)
-    down = jnp.full((1, 1), 1.0 / 64.0, jnp.float32)
-    for e in (32, 16, 8, 4, 2, 1):
-        fits = biggest * up * (2.0**e) <= 448.0
-        up = jnp.where(fits, up * (2.0**e), up)
-        down = jnp.where(fits, down * (2.0**-e), down)
     line = lax.broadcasted_iota(jnp.int32, (8, KC), 0)
     for at in range(0, rows, KC):
-        g = grad[:, at : at + KC] * up
-        h = hess[:, at : at + KC] * 256.0
-        both = jnp.where(line % 2 == 0, jnp.broadcast_to(g, (8, KC)), jnp.broadcast_to(h, (8, KC)))
-        first = both.astype(F8).astype(jnp.float32)
-        second = (both - first) * 16.0
+        grad = jnp.broadcast_to(grad_ref[:, at : at + KC].astype(jnp.float32), (8, KC))
+        hess = jnp.broadcast_to(hess_ref[:, at : at + KC].astype(jnp.float32), (8, KC))
+        both = jnp.where(line % 2 == 0, grad, hess)
         fold = fold_ref[:, at : at + KC]
-        pieces = [[], []]
+        made = []
         for k in range(FOLDS):
-            node = nodes_ref[k : k + 1, at : at + KC]
-            node = jnp.where(fold == k, -1, node)
-            sel = jnp.broadcast_to(node, (8, KC)) == line // 2
-            pieces[0].append(jnp.where(sel, first, 0.0))
-            pieces[1].append(jnp.where(sel, second, 0.0))
-        every = pieces[0] + pieces[1]
-        for q in range(0, 2 * FOLDS, 4):
-            w_ref[q * 8 : q * 8 + 32, at : at + KC] = jnp.concatenate(every[q : q + 4], axis=0).astype(F8)
-    return down
-
-
-def histogram(bins_ref, w_ref, loc_ref, slot, first, scale):
+            node = jnp.where(fold == k, -1, nodes_ref[k : k + 1, at : at + KC])
+            made.append(jnp.where(jnp.broadcast_to(node, (8, KC)) == line // 2, both, 0.0))
+        for q in range(0, FOLDS, 2):
+            w_ref[q * 8 : q * 8 + 16, at : at + KC] = jnp.concatenate(made[q : q + 2], axis=0).astype(jnp.bfloat16)
+
+
+def histogram(bins_ref, w_ref, loc_ref, slot, first):
     rows = w_ref.shape[1]
     level = lax.broadcasted_iota(jnp.int32, (BINS, 1), 0).astype(jnp.float32).astype(jnp.bfloat16)
     for f in range(NF):
@@ -69,9 +53,8 @@
                 w_ref[:, at : at + KC], hot, (((1,), (1,)), ((), ())), preferred_element_type=jnp.float32
             )
             total = term if total is None else total + term
-        hist = (total[:COLS] + total[COLS:] * (1.0 / 16.0)) * scale
         for part in range(HALVES):
-            loc_ref[slot, part, pl.ds(f, COLS, stride=NF), :] = hist[:, part * LANES : (part + 1) * LANES]
+            loc_ref[slot, part, pl.ds(f, COLS, stride=NF), :] = total[:, part * LANES : (part + 1) * LANES]
 
 
 def gains(done):
@@ -167,15 +150,13 @@
         )[k]()
         return send(src, dst, (ys, yr), i, k, to)
 
-    down = build_weights(fold_ref, nodes_ref, grad_ref, hess_ref, w_ref)
-    column = lax.broadcasted_iota(jnp.int32, (COLS, BINS), 0)
-    scale = jnp.where(column % 2 == 0, jnp.broadcast_to(down, (COLS, BINS)), 1.0 / 256.0)
+    build_weights(fold_ref, nodes_ref, grad_ref, hess_ref, w_ref)
     most[...] = jnp.full(most.shape, LOW, jnp.float32)
 
     def visit(i, carry):
         @pl.when(i < pairs)
         def _():
-            histogram(bins_ref, w_ref, locx, i, 2 * NF * i, scale)
+            histogram(bins_ref, w_ref, locx, i, 2 * NF * i)
 
             @pl.when(i == 0)
             def _():
@@ -183,7 +164,7 @@
 
             for k in range(4):
                 x_copy(i, k).start()
-            histogram(bins_ref, w_ref, locy, i, 2 * NF * i + NF, scale)
+            histogram(bins_ref, w_ref, locy, i, 2 * NF * i + NF)
             y_copy(i, 0).start()
 
         @pl.when((i >= 1) & (i < pairs + 1))
@@ -298,7 +279,7 @@
         in_specs=[vmem] * 5,
         out_specs=(vmem, vmem),
         scratch_shapes=[
-            pltpu.VMEM((2 * COLS, rows_here), F8),
+            pltpu.VMEM((COLS, rows_here), jnp.bfloat16),
             pltpu.VMEM((pairs, HALVES, COLS * NF, LANES), f32),
             pltpu.VMEM((pairs, HALVES, COLS * NF, LANES), f32),
             pltpu.VMEM((pairs, 2, HALVES, BLK, LANES), f32),

time: 61.7 us -> 62.3 us (level)
  no operation moved by 1% of the time
where the time goes in v2:
time: 62.3 us; the launch traced here: 62 us
  Pallas kernels  56.4 us (91%)
  local copies, waits for them, and re-layouts  4.94 us (8%)
  between operations  0.68 us (1%)
    pallas_call x1, Pallas kernels, on_device(): pl.pallas_call(functools.partial(kernel, pairs, feats_way), out_shape=(ja...  56.4 us
    unnamed x9, local copies, waits for them, and re-layouts  3.56 us

profile of v2, /device:TPU:1, one launch (start us, length us, event | category | flops | bytes accessed | tf_op | source)
XLA Modules:
  0.0 62.0 jit_solution(6629305481268690030)
XLA Ops:
  0.6 0.0 copy-start.3
  0.6 0.7 %reshape.14.grad_ref = bf16[1,4096]{1,0:T(2,128)(2,1)S(1)} reshape(bf16[4096]{0:T(1024)(128)(2,1)} %param.8) | data formatting | bytes 16384 | tf_op jit(solution)/shard_map/reshape | solution.py:301
  1.4 0.0 copy-done.3
  1.4 0.0 copy-start.2
  1.4 0.7 %copy-done.2 = s32[4096]{0:T(1024)S(1)} copy-done((s32[4096]{0:T(1024)S(1)}, s32[4096]{0:T(1024)}, u32[]{:S(2)}) %copy-start.2) | copy-done | bytes 16408
  2.1 0.0 copy-start
  2.1 1.1 %copy-done = s32[48,4096]{1,0:T(8,128)S(1)} copy-done((s32[48,4096]{1,0:T(8,128)S(1)}, s32[48,4096]{1,0:T(8,128)}, u32[]{:S(2)}) %copy-start) | copy-done | bytes 786456
  3.2 0.0 copy-start.1
  3.2 0.9 %copy-done.1 = s32[4096,10]{0,1:T(8,128)S(1)} copy-done((s32[4096,10]{0,1:T(8,128)S(1)}, s32[4096,10]{0,1:T(8,128)}, u32[]{:S(2)}) %copy-start.1) | copy-done | bytes 163864
  4.2 56.4 %shard_map.68 = (f32[10,48,256]{2,1,0:T(8,128)S(1)}, f32[10,4]{1,0:T(8,128)S(1)}) custom-call(s32[48,4096]{1,0:T(8,128)S(1)} %copy-done, s32[1,4096]{1,0:T(1,128)S(1)} %bitcast.3, s32[10,4096]{1,0:T(8,128)S(1)} %bitcast.2, bf16[1,4096]{1,0:T(2,128)(2,1)S(1)} %reshape.14.grad_ref, bf16[1,4096]{1,0:T(2,128)(2,1)S(1)} %reshape.15.hess_ref), custom_call_target="tpu_custom_call" | custom-call | tf_op jit(solution)/shard_map/pallas_call | solution.py:273
  60.6 0.7 %copy.7 = f32[10,4]{0,1:T(4,128)} copy(f32[10,4]{1,0:T(8,128)S(1)} %get-tuple-element.3) | data formatting | bytes 320 | tf_op jit(solution)/shard_map/pallas_call | solution.py:273
  61.2 0.8 %copy.9 = f32[10,48,256]{2,1,0:T(8,128)} copy(f32[10,48,256]{2,1,0:T(8,128)S(1)} %get-tuple-element.6) | data formatting | bytes 983040
  (1 shorter events, 0.0 us)
Async XLA Ops:
  0.6 0.7 %copy-start.3 = (bf16[4096]{0:T(1024)(128)(2,1)S(1)}, bf16[4096]{0:T(1024)(128)(2,1)}, u32[]{:S(2)}) copy-start(bf16[4096]{0:T(1024)(128)(2,1)} %param.9) | copy-start | bytes 24580
  1.4 0.7 %copy-start.2 = (s32[4096]{0:T(1024)S(1)}, s32[4096]{0:T(1024)}, u32[]{:S(2)}) copy-start(s32[4096]{0:T(1024)} %param.6) | copy-start | bytes 49156
  2.1 1.1 %copy-start = (s32[48,4096]{1,0:T(8,128)S(1)}, s32[48,4096]{1,0:T(8,128)}, u32[]{:S(2)}) copy-start(s32[48,4096]{1,0:T(8,128)} %bins_ref.1) | copy-start | bytes 2359300
  3.2 0.9 %copy-start.1 = (s32[4096,10]{0,1:T(8,128)S(1)}, s32[4096,10]{0,1:T(8,128)}, u32[]{:S(2)}) copy-start(s32[4096,10]{0,1:T(8,128)} %param.7) | copy-start | bytes 491524

commit v3 on v0

v3 whole, which is shorter than its diff:
```python
import functools

import jax
import jax.numpy as jnp
from jax import lax
from jax.experimental import pallas as pl
from jax.experimental.pallas import tpu as pltpu
from jax.sharding import PartitionSpec as P

BINS = 256
FOLDS = 10
NODES = 4
COLS = FOLDS * NODES * 2
X = 4
Y = 2
OWN = COLS // (X * Y)
NF = 4
BLK = OWN * NF
CUT = 24
F8 = jnp.float8_e4m3fn
MESH = pl.DeviceIdType.MESH
LOW = -1e30
LANES = 128
HALVES = BINS // LANES
KC = 512
KINDS = "xxxxxxxxgggg"
LAGS = {"x": (3, 6, 9), "y": (5, 7, 8), "g": (3,)}


def chosen(nodes, grad, hess):
    line = lax.broadcasted_iota(jnp.int32, (8, LANES), 0)
    both = jnp.where(line % 2 == 0, jnp.broadcast_to(grad, (8, LANES)), jnp.broadcast_to(hess, (8, LANES)))
    which = (line // 2).astype(nodes[0].dtype)
    return [jnp.where(jnp.broadcast_to(node, (8, LANES)) == which, both, 0.0) for node in nodes]


def build_weights(y, fold_ref, nodes_ref, grad_ref, hess_ref, w_ref, half_ref, letter_ref):
    grads = grad_ref[...].astype(jnp.float32)
    hesses = hess_ref[...].astype(jnp.float32)
    some = FOLDS // Y
    for j in range(w_ref.shape[1] // LANES):
        at = slice(j * LANES, (j + 1) * LANES)
        grad, hess, fold = grads[j : j + 1], hesses[j : j + 1], fold_ref[j : j + 1, :]

        nodes = [jnp.where(fold == k, -1, nodes_ref[k : k + 1, at]) for k in range(FOLDS)]
        made = chosen(nodes, grad, hess)
        for q in range(0, FOLDS, 2):
            w_ref[q * 8 : q * 8 + 16, at] = jnp.concatenate(made[q : q + 2], axis=0).astype(jnp.bfloat16)
        made = [jnp.where(y == 0, made[i], made[some + i]) for i in range(some)]
        half_ref[0, :, at] = jnp.concatenate(made, axis=0).astype(jnp.bfloat16)
        for i in range(some):
            letter_ref[i : i + 1, at] = jnp.where(y == 0, nodes[some + i], nodes[i]).astype(jnp.float32)
        letter_ref[some : some + 1, at] = grad
        letter_ref[some + 1 : some + 2, at] = hess


def read_letter(letter_ref, half_ref):
    some = FOLDS // Y
    for j in range(letter_ref.shape[1] // LANES):
        at = slice(j * LANES, (j + 1) * LANES)
        nodes = [letter_ref[i : i + 1, at] for i in range(some)]
        made = chosen(nodes, letter_ref[some : some + 1, at], letter_ref[some + 1 : some + 2, at])
        half_ref[1, :, at] = jnp.concatenate(made, axis=0).astype(jnp.bfloat16)


def histogram(parts, into_ref):
    level = lax.broadcasted_iota(jnp.int32, (BINS, 1), 0).astype(jnp.float32).astype(jnp.bfloat16)

    def one(f, carry):
        total = None
        for bins_ref, first, w_ref in parts:
            for at in range(0, w_ref.shape[1], KC):
                b = bins_ref[pl.ds(first + f, 1), at : at + KC].astype(jnp.float32).astype(jnp.bfloat16)
                hot = jnp.where(b == level, jnp.bfloat16(1), jnp.bfloat16(0)).astype(F8)
                term = lax.dot_general(
                    w_ref[:, at : at + KC], hot, (((1,), (1,)), ((), ())), preferred_element_type=jnp.float32
                )
                total = term if total is None else total + term
        for half in range(HALVES):
            into_ref[half, pl.ds(f, total.shape[0], stride=NF), :] = total[:, half * LANES : (half + 1) * LANES]
        return carry

    lax.fori_loop(0, NF, one, 0)


def gains(done):
    lane = lax.broadcasted_iota(jnp.int32, (BLK, BINS), 1)
    line = lax.broadcasted_iota(jnp.int32, (BLK, BINS), 0)
    left = done
    step = 1
    while step < BINS:
        left = left + jnp.where(lane >= step, pltpu.roll(left, step, 1), 0.0)
        step *= 2
    whole = jnp.broadcast_to(left[:, BINS - 1 :], (BLK, BINS))
    left_h = pltpu.roll(left, BLK - NF, 0)
    whole_h = pltpu.roll(whole, BLK - NF, 0)
    good = (line % (2 * NF) < NF) & (lane < BINS - 1)
    left_h = jnp.where(good, left_h, 0.0)
    whole_h = jnp.where(good, whole_h, 0.0)
    gain = (
        left * left / (left_h + 1.0)
        + (whole - left) * (whole - left) / (whole_h - left_h + 1.0)
        - whole * whole / (whole_h + 1.0)
    )
    return jnp.where(good, gain, LOW)


def plan(chunks):
    counts = {"x": 0, "y": 0, "g": 0}
    order, events = [], []
    alone = len(KINDS) - KINDS.count("g")
    for c, kind in enumerate(KINDS):
        place = alone + counts["g"] if kind == "g" else counts["x"] + counts["y"]
        order.append((kind, counts[kind], place * NF))
        counts[kind] += 1
        for step, lag in enumerate(LAGS[kind]):
            events.append((c + lag, c, step + 1))
    return order, sorted(events), counts


def kernel(
    feats, feats_way,
    bins_hbm, fold_hbm, nodes_hbm, grad_hbm, hess_hbm,
    hist_ref, best_ref,
    bins_ref, fold_ref, nodes_ref, grad_ref, hess_ref,
    w_ref, half_ref, letter_out, letter_in, bins_in, loc, r1, r2, r3, y1, y2, y3, rg, most, mine_ref, core_in, near_in, far_in,
    get, ps, pr, es, er, cs, cr, ns, nr, fs, fr,
):
    row = lax.axis_index("rows")
    feat = lax.axis_index("feat")
    y, x = row // X, row % X
    around = X * Y
    chips = feats_way // 2
    chip, core = feat // 2, feat % 2
    order, events, _ = plan(feats // NF)

    barrier = pltpu.get_barrier_semaphore()

    def to_row(d):
        return {"rows": (row + d) % around}

    def to_chip(d):
        return {"feat": (chip + d) % chips * 2 + core}

    to_core = {"feat": chip * 2 + 1 - core}
    for d in range(1, around):
        pl.semaphore_signal(barrier, inc=1, device_id=to_row(d), device_id_type=MESH)
    for d in range(1, chips):
        pl.semaphore_signal(barrier, inc=1, device_id=to_chip(d), device_id_type=MESH)
    pl.semaphore_signal(barrier, inc=1, device_id=to_core, device_id_type=MESH)

    pairs = ((nodes_hbm, nodes_ref), (fold_hbm, fold_ref), (grad_hbm, grad_ref), (hess_hbm, hess_ref), (bins_hbm, bins_ref))
    gets = [pltpu.make_async_copy(src, dst, get.at[i]) for i, (src, dst) in enumerate(pairs)]
    for g in gets:
        g.start()

    right = {"rows": y * X + (x + 1) % X}
    left = {"rows": y * X + (x + X - 1) % X}
    over = {"rows": (Y - 1 - y) * X + x}

    def spot(yy, xx, start=0):
        return pl.multiple_of((yy * X + xx % X) * BLK + start, 8)

    def send(src, dst, sems, k, to):
        return pltpu.make_async_remote_copy(
            src_ref=src, dst_ref=dst, send_sem=sems[0].at[k], recv_sem=sems[1].at[k],
            device_id=to, device_id_type=MESH,
        )

    def rows_of(c, at, size):
        return loc.at[c, :, pl.ds(at, size)]

    def copy(c, k):
        kind, i, base = order[c]

        def part(yy, xx, a=0, b=BLK):
            return rows_of(c, spot(yy, xx, a), b - a)

        def cut(ref, a, b):
            return ref.at[:, pl.ds(a, b - a)]

        if kind == "g":
            there = (x + k + 1) % X
            src = rows_of(c, pl.multiple_of(there * BLK, 8), BLK)
            return send(src, rg.at[i, k], (ps.at[c], pr.at[c]), k, {"rows": y * X + there})
        if kind == "x":
            src, dst, to = (
                lambda: (part(0, x + 2), r1.at[i, 0], right),
                lambda: (part(1, x + 2), r1.at[i, 1], left),
                lambda: (part(1, x + 1), r2.at[i, 1], right),
                lambda: (part(0, x + 3), r2.at[i, 2], left),
                lambda: (part(0, x + 1), r2.at[i, 0], right),
                lambda: (part(1, x + 3), r2.at[i, 3], left),
                lambda: (part(Y - 1 - y, x), r3.at[i], over),
            )[k]()
        else:
            src, dst, to = (
                lambda: (rows_of(c, spot(Y - 1 - y, 0), X * BLK), y1.at[i], over),
                lambda: (part(y, x + 2, 0, CUT), cut(y2.at[i], 0, CUT), right),
                lambda: (part(y, x + 2, CUT, BLK), cut(y2.at[i], CUT, BLK), left),
                lambda: (part(y, x + 1, CUT, BLK), cut(y3.at[i, 0], CUT, BLK), right),
                lambda: (part(y, x + 3, 0, CUT), cut(y3.at[i, 1], 0, CUT), left),
                lambda: (part(y, x + 1, 0, CUT), cut(y3.at[i, 0], 0, CUT), right),
                lambda: (part(y, x + 3, CUT, BLK), cut(y3.at[i, 1], CUT, BLK), left),
            )[k]()
        return send(src, dst, (ps.at[c], pr.at[c]), k, to)

    def start(c, ks):
        for k in ks:
            copy(c, k).start()

    def arrive(c, ks):
        for k in ks:
            copy(c, k).wait_recv()

    def grow(c, at, size, *terms):
        total = terms[0]
        for term in terms[1:]:
            total = total + term
        loc[c, :, pl.ds(at, size), :] += total

    def finish(c, *terms):
        kind, i, base = order[c]
        at = pl.multiple_of(x * BLK, 8) if kind == "g" else spot(y, x)
        done = loc[c, :, pl.ds(at, BLK), :]
        for term in terms:
            done = done + term
        done = jnp.concatenate([done[half] for half in range(HALVES)], axis=1)
        for col in range(OWN):
            hist_ref[col, base : base + NF, :] = done[col * NF : (col + 1) * NF]
        most[...] = jnp.maximum(most[...], gains(done))

    def advance(c, step):
        kind, i, base = order[c]
        if kind == "g":
            arrive(c, range(X - 1))
            finish(c, *[rg[i, d] for d in range(X - 1)])
        elif kind == "x" and step == 1:
            arrive(c, (0, 1))
            grow(c, spot(0, x + 1), BLK, r1[i, 0])
            grow(c, spot(1, x + 3), BLK, r1[i, 1])
            start(c, (2, 3, 4, 5))
        elif kind == "x" and step == 2:
            arrive(c, (2, 3, 4, 5))
            grow(c, spot(Y - 1 - y, x), BLK, r2[i, Y - 1 - y], r2[i, Y + Y - 1 - y])
            start(c, (6,))
            grow(c, spot(y, x), BLK, r2[i, y], r2[i, Y + y])
        elif kind == "x":
            arrive(c, (6,))
            finish(c, r3[i])
        elif step == 1:
            arrive(c, (0,))
            grow(c, spot(y, 0), X * BLK, y1[i])
            start(c, (1, 2))
        elif step == 2:
            arrive(c, (1, 2))
            grow(c, spot(y, x + 1), CUT, y2[i, :, pl.ds(0, CUT), :])
            grow(c, spot(y, x + 3, CUT), BLK - CUT, y2[i, :, pl.ds(CUT, BLK - CUT), :])
            start(c, (3, 4, 5, 6))
        else:
            arrive(c, (3, 4, 5, 6))
            finish(c, y3[i, 0], y3[i, 1])

    for g in gets[:4]:
        g.wait()
    build_weights(y, fold_ref, nodes_ref, grad_ref, hess_ref, w_ref, half_ref, letter_out)
    most[...] = jnp.full(most.shape, LOW, jnp.float32)
    gets[4].wait()

    shared = (len(KINDS) - KINDS.count("g")) * NF
    swaps = [send(letter_out, letter_in, (es, er), 0, over)]
    for i in range((feats - shared) // 8):
        swaps.append(
            send(bins_ref.at[pl.ds(shared + 8 * i, 8)], bins_in.at[pl.ds(8 * i, 8)], (es, er), i + 1, over)
        )
    todo = list(events)
    for c, (kind, i, base) in enumerate(order):
        if kind == "g" and i == 0:
            swaps[0].wait_recv()
            read_letter(letter_in, half_ref)
        if kind == "g" and i % 2 == 0:
            swaps[1 + i // 2].wait_recv()
        if kind == "g":
            histogram(((bins_ref, base, half_ref.at[0]), (bins_in, i * NF, half_ref.at[1])), loc.at[c])
        else:
            histogram(((bins_ref, base, w_ref),), loc.at[c])
        if c == 0:
            pl.semaphore_wait(barrier, around - 1 + chips - 1 + 1)
            for e in swaps:
                e.start()
        start(c, {"x": (0, 1), "y": (0,), "g": range(X - 1)}[kind])
        while todo and todo[0][0] <= c:
            advance(*todo.pop(0)[1:])
    for _, c, step in todo:
        advance(c, step)

    lane = lax.broadcasted_iota(jnp.int32, (1, LANES), 1)
    mine = jnp.full((1, LANES), LOW, jnp.float32)
    for m in range(OWN // 2):
        part = most[m * 2 * NF : (m + 1) * 2 * NF, :]
        part = jnp.max(jnp.max(part, axis=1, keepdims=True), axis=0, keepdims=True)
        mine = jnp.where(lane == row * (OWN // 2) + m, jnp.broadcast_to(part, (1, LANES)), mine)

    mine_ref[0] = mine
    swap = send(mine_ref.at[0], core_in.at[0], (cs, cr), 0, to_core)
    swap.start()
    swap.wait_recv()
    mine = jnp.maximum(mine, core_in[0])
    mine_ref[1] = mine
    near = [send(mine_ref.at[1], near_in.at[d], (ns, nr), d, to_chip(d)) for d in range(1, chips)]
    for n in near:
        n.start()
    for c, (kind, i, base) in enumerate(order):
        for k in range(X - 1 if kind == "g" else 7):
            copy(c, k).wait_send()
    for n in near:
        n.wait_recv()
    for d in range(1, chips):
        mine = jnp.maximum(mine, near_in[d])
    mine_ref[2] = mine
    far = [send(mine_ref.at[2], far_in.at[d], (fs, fr), d, to_row(d)) for d in range(1, around)]
    for n in far:
        n.start()
    for n in far:
        n.wait_recv()
    for d in range(1, around):
        mine = jnp.maximum(mine, far_in[d])
    for k in range(FOLDS):
        best_ref[k : k + 1, :] = mine[0:1, k * NODES : (k + 1) * NODES]
    for n in [swap] + swaps + near + far:
        n.wait_send()


def on_device(bins, fold, nodes, gradient, hessian):
    feats, rows_here = bins.shape
    chunks = feats // NF
    counts = plan(chunks)[2]
    feats_way = lax.axis_size("feat")
    around = X * Y
    f32 = jnp.float32
    dma = pltpu.SemaphoreType.DMA
    vmem = pl.BlockSpec(memory_space=pltpu.VMEM)
    stay = pl.BlockSpec(memory_space=pltpu.HBM)
    lines = rows_here // LANES
    return pl.pallas_call(
        functools.partial(kernel, feats, feats_way),
        out_shape=(
            jax.ShapeDtypeStruct((OWN, feats, BINS), f32),
            jax.ShapeDtypeStruct((FOLDS, NODES), f32),
        ),
        in_specs=[stay] * 5,
        out_specs=(vmem, vmem),
        scratch_shapes=[
            pltpu.VMEM((feats, rows_here), jnp.int32),
            pltpu.VMEM((lines, LANES), jnp.int32),
            pltpu.VMEM((FOLDS, rows_here), jnp.int32),
            pltpu.VMEM((lines, LANES), jnp.bfloat16),
            pltpu.VMEM((lines, LANES), jnp.bfloat16),
            pltpu.VMEM((COLS, rows_here), jnp.bfloat16),
            pltpu.VMEM((2, COLS // Y, rows_here), jnp.bfloat16),
            pltpu.VMEM((8, rows_here), f32),
            pltpu.VMEM((8, rows_here), f32),
            pltpu.VMEM((counts["g"] * NF, rows_here), jnp.int32),
            pltpu.VMEM((chunks, HALVES, COLS * NF, LANES), f32),
            pltpu.VMEM((max(counts["x"], 1), 2, HALVES, BLK, LANES), f32),
            pltpu.VMEM((max(counts["x"], 1), 4, HALVES, BLK, LANES), f32),
            pltpu.VMEM((max(counts["x"], 1), HALVES, BLK, LANES), f32),
            pltpu.VMEM((max(counts["y"], 1), HALVES, X * BLK, LANES), f32),
            pltpu.VMEM((max(counts["y"], 1), HALVES, BLK, LANES), f32),
            pltpu.VMEM((max(counts["y"], 1), 2, HALVES, BLK, LANES), f32),
            pltpu.VMEM((counts["g"], X - 1, HALVES, BLK, LANES), f32),
            pltpu.VMEM((BLK, BINS), f32),
            pltpu.VMEM((3, 1, LANES), f32),
            pltpu.VMEM((1, 1, LANES), f32),
            pltpu.VMEM((feats_way // 2, 1, LANES), f32),
            pltpu.VMEM((around, 1, LANES), f32),
            dma((5,)),
            dma((chunks, 7)), dma((chunks, 7)),
            dma((1 + chunks // 2,)), dma((1 + chunks // 2,)),
            dma((1,)), dma((1,)),
            dma((feats_way // 2,)), dma((feats_way // 2,)),
            dma((around,)), dma((around,)),
        ],
        compiler_params=pltpu.CompilerParams(
            collective_id=0, has_side_effects=True, vmem_limit_bytes=48 << 20
        ),
    )(*[
        pltpu.with_memory_space_constraint(a, pltpu.HBM)
        for a in (bins, fold.reshape(lines, LANES), nodes.T, gradient.reshape(lines, LANES), hessian.reshape(lines, LANES))
    ])


def solution(mesh):
    in_specs = (P("feat", "rows"), P("rows"), P("rows", None), P("rows"), P("rows"))
    out_specs = (P("rows", "feat", None), P())
    return jax.shard_map(
        on_device, mesh=mesh, in_specs=in_specs, out_specs=out_specs, check_vma=False
    )
```

time: 256 us -> 58.2 us (0.23)
  matrix products: 101 us -> 0 us
  waiting for transfers between devices: 85.9 us -> 0 us
  Pallas kernels: 0 us -> 56 us
  blocking collectives: 23.9 us -> 0 us
  local copies, waits for them, and re-layouts: 20.5 us -> 1.44 us
  between operations: 14.2 us -> 0.64 us
  other arithmetic: 9.27 us -> 0 us
    dot_general x24 -> x0, matrix products: 101 us -> none  [visit(): jnp.einsum('cr,fbr->cfb', part_weights, onehot, preferred_element_type=jn...]
    reduce_scatter x1 -> x0, waiting for transfers between devices: 85.9 us -> none  [on_device(): reduced = lax.psum_scatter(local, 'rows', scatter_dimension=0, tiled=True)]
    pallas_call x0 -> x1, Pallas kernels: none -> 56 us  [on_device(): pl.pallas_call(functools.partial(kernel, feats, feats_way), out_shape=(ja...]
    all_to_all x2 -> x0, blocking collectives: 23.9 us -> none  [from_everyone(): return lax.all_to_all(copies, axis, split_axis=0, concat_axis=0, tiled=True)]
    another operation x6 -> x0, other arithmetic: 7.22 us -> none
    slice x9 -> x0, local copies, waits for them, and re-layouts: 6.55 us -> none  [the longest x8 6.37 us: visit(): part_bins[first:first + group, None, :] == levels[None]]
    while x1 -> x0, local copies, waits for them, and re-layouts: 6.29 us -> none  [accumulate(): return lax.fori_loop(0, rows_here // block, visit, empty)]
  transfers between devices with their start and end apart: 1 -> 0, of which waited for: 1 -> 0; matrix products, arithmetic and copies ran while one was open for 0% -> 0% of each run, Pallas kernels for 0% -> 0%
where the time goes in v3:
time: 58.2 us; the launch traced here: 58 us
  Pallas kernels  56 us (96%)
  local copies, waits for them, and re-layouts  1.44 us (2%)
  between operations  0.64 us (1%)
    pallas_call x1, Pallas kernels, on_device(): pl.pallas_call(functools.partial(kernel, feats, feats_way), out_shape=(ja...  56 us

profile of v3, /device:TPU:1, one launch (start us, length us, event | category | flops | bytes accessed | tf_op | source)
XLA Modules:
  0.0 58.0 jit_solution(5554162430032279058)
XLA Ops:
  0.6 56.0 %shard_map.68 = (f32[10,48,256]{2,1,0:T(8,128)S(1)}, f32[10,4]{1,0:T(8,128)S(1)}) custom-call(s32[48,4096]{1,0:T(8,128)} %bins_hbm.1, s32[32,128]{1,0:T(8,128)} %bitcast.5, s32[10,4096]{1,0:T(8,128)} %bitcast.4, bf16[32,128]{1,0:T(8,128)(2,1)} %bitcast.6, bf16[32,128]{1,0:T(8,128)(2,1)} %bitcast.7), custom_call_target="tpu_custom_call" | custom-call | tf_op jit(solution)/shard_map/pallas_call | solution.py:345
  56.6 0.7 %copy.7 = f32[10,4]{0,1:T(4,128)} copy(f32[10,4]{1,0:T(8,128)S(1)} %get-tuple-element.3) | data formatting | bytes 320 | tf_op jit(solution)/shard_map/pallas_call | solution.py:345
  57.3 0.8 %copy.9 = f32[10,48,256]{2,1,0:T(8,128)} copy(f32[10,48,256]{2,1,0:T(8,128)S(1)} %get-tuple-element.6) | data formatting | bytes 983040

commit v4 on v3

--- a/solution.py
+++ b/solution.py
@@ -80,7 +80,7 @@
             into_ref[half, pl.ds(f, total.shape[0], stride=NF), :] = total[:, half * LANES : (half + 1) * LANES]
         return carry
 
-    lax.fori_loop(0, NF, one, 0)
+    lax.fori_loop(0, NF, one, 0, unroll=4)
 
 
 def gains(done):

time: 58.2 us -> 56.8 us (0.976)
  Pallas kernels: 56 us -> 54.6 us
    pallas_call x1, Pallas kernels: 56 us -> 54.6 us  [on_device(): pl.pallas_call(functools.partial(kernel, feats, feats_way), out_shape=(ja...]
where the time goes in v4:
time: 56.8 us; the launch traced here: 56.7 us
  Pallas kernels  54.6 us (96%)
  local copies, waits for them, and re-layouts  1.44 us (3%)
  between operations  0.64 us (1%)
    pallas_call x1, Pallas kernels, on_device(): pl.pallas_call(functools.partial(kernel, feats, feats_way), out_shape=(ja...  54.6 us

profile of v4, /device:TPU:1, one launch (start us, length us, event | category | flops | bytes accessed | tf_op | source)
XLA Modules:
  0.0 56.7 jit_solution(2845979967182545175)
XLA Ops:
  0.6 54.6 %shard_map.68 = (f32[10,48,256]{2,1,0:T(8,128)S(1)}, f32[10,4]{1,0:T(8,128)S(1)}) custom-call(s32[48,4096]{1,0:T(8,128)} %bins_hbm.1, s32[32,128]{1,0:T(8,128)} %bitcast.5, s32[10,4096]{1,0:T(8,128)} %bitcast.4, bf16[32,128]{1,0:T(8,128)(2,1)} %bitcast.6, bf16[32,128]{1,0:T(8,128)(2,1)} %bitcast.7), custom_call_target="tpu_custom_call" | custom-call | tf_op jit(solution)/shard_map/pallas_call | solution.py:345
  55.3 0.7 %copy.7 = f32[10,4]{0,1:T(4,128)} copy(f32[10,4]{1,0:T(8,128)S(1)} %get-tuple-element.3) | data formatting | bytes 320 | tf_op jit(solution)/shard_map/pallas_call | solution.py:345
  55.9 0.8 %copy.9 = f32[10,48,256]{2,1,0:T(8,128)} copy(f32[10,48,256]{2,1,0:T(8,128)S(1)} %get-tuple-element.6) | data formatting | bytes 983040

commit v5 on v4

--- a/solution.py
+++ b/solution.py
@@ -239,7 +239,7 @@
             arrive(c, (0, 1))
             grow(c, spot(0, x + 1), BLK, r1[i, 0])
             grow(c, spot(1, x + 3), BLK, r1[i, 1])
-            start(c, (2, 3, 4, 5))
+            start(c, (4, 5))
         elif kind == "x" and step == 2:
             arrive(c, (2, 3, 4, 5))
             grow(c, spot(Y - 1 - y, x), BLK, r2[i, Y - 1 - y], r2[i, Y + Y - 1 - y])
@@ -288,7 +288,7 @@
             pl.semaphore_wait(barrier, around - 1 + chips - 1 + 1)
             for e in swaps:
                 e.start()
-        start(c, {"x": (0, 1), "y": (0,), "g": range(X - 1)}[kind])
+        start(c, {"x": (0, 1, 2, 3), "y": (0,), "g": range(X - 1)}[kind])
         while todo and todo[0][0] <= c:
             advance(*todo.pop(0)[1:])
     for _, c, step in todo:

time: 56.8 us -> 55.8 us (0.982)
  Pallas kernels: 54.6 us -> 53.6 us
    pallas_call x1, Pallas kernels: 54.6 us -> 53.6 us  [on_device(): pl.pallas_call(functools.partial(kernel, feats, feats_way), out_shape=(ja...]
where the time goes in v5:
time: 55.8 us; the launch traced here: 55.7 us
  Pallas kernels  53.6 us (96%)
  local copies, waits for them, and re-layouts  1.44 us (3%)
  between operations  0.64 us (1%)
    pallas_call x1, Pallas kernels, on_device(): pl.pallas_call(functools.partial(kernel, feats, feats_way), out_shape=(ja...  53.6 us

profile of v5, /device:TPU:1, one launch (start us, length us, event | category | flops | bytes accessed | tf_op | source)
XLA Modules:
  0.0 55.7 jit_solution(1748475233694514442)
XLA Ops:
  0.6 53.6 %shard_map.68 = (f32[10,48,256]{2,1,0:T(8,128)S(1)}, f32[10,4]{1,0:T(8,128)S(1)}) custom-call(s32[48,4096]{1,0:T(8,128)} %bins_hbm.1, s32[32,128]{1,0:T(8,128)} %bitcast.5, s32[10,4096]{1,0:T(8,128)} %bitcast.4, bf16[32,128]{1,0:T(8,128)(2,1)} %bitcast.6, bf16[32,128]{1,0:T(8,128)(2,1)} %bitcast.7), custom_call_target="tpu_custom_call" | custom-call | tf_op jit(solution)/shard_map/pallas_call | solution.py:345
  54.3 0.7 %copy.7 = f32[10,4]{0,1:T(4,128)} copy(f32[10,4]{1,0:T(8,128)S(1)} %get-tuple-element.3) | data formatting | bytes 320 | tf_op jit(solution)/shard_map/pallas_call | solution.py:345
  54.9 0.8 %copy.9 = f32[10,48,256]{2,1,0:T(8,128)} copy(f32[10,48,256]{2,1,0:T(8,128)S(1)} %get-tuple-element.6) | data formatting | bytes 983040
